TPU v7x, 32 devices: a whole 2x2x4 slice. The times are simulated.
32 devices in a mesh: ord: 8 (over y, x, core), ch: 4 (over z).
Axes of the slice: x: 2, y: 2, z: 4, core: 2. Of those that a mesh axis runs over, the one named last changes fastest.
Arguments:
- field_grid: bfloat16 [2, 64, 2, 352, 1440], P(None, 'ch', None, 'ord'), may hold values from -40 to 40
- norm_gain: float32 [64], P('ch'), may hold values from 0.1 to 1.9
- norm_bias: float32 [64], P('ch'), may hold values from -3 to 3
- order_table: int32 [512], replicated, may hold values from 0 to 511, as said below
- legendre: bfloat16 [512, 2, 352, 360], P(('ord', 'ch')), may hold values from -0.3125 to 0.3125
Outputs:
- coefficients: bfloat16 [512, 2, 2, 2, 64, 360], P(('ord', 'ch'))
Inputs may be any that keep to these rules, and one draw needn't show every extreme that they name: `order_table`: a permutation of the orders in which slots 2 q and 2 q + 1 hold orders p and 511 - p.
All inputs are finite; a program needn't handle non-finite values.
Results may differ from a plain program's by a relative error of at most 0.0062.
Values may be sent and summed in bfloat16 or wider, within the bound.
A program may use at most 128 MiB of HBM per device.

v0:
```python
from functools import partial
import math

import jax
import jax.numpy as jnp
from jax import lax
from jax.experimental import pallas as pl
from jax.experimental.pallas import tpu as pltpu
from jax.sharding import PartitionSpec as P

MESH = pl.DeviceIdType.MESH
LANES = 128
GROUP = 128
QUAD = 4
PITCH = 40


def slot_table(orders, length):
    sample = jnp.arange(length, dtype=jnp.int32)
    phases = sample[:, None] * orders[None, :] % length
    angles = phases.astype(jnp.float32) * (2.0 * math.pi / length)
    factor = 1.0 / math.sqrt(length)
    stacked = jnp.stack([jnp.cos(angles) * factor, -jnp.sin(angles) * factor], axis=2)
    return stacked.reshape(length, 2 * orders.shape[0]).astype(jnp.bfloat16)


def legendre_sums(arrived, legendre, orders):
    odd_order = orders % 2 == 1
    swapped = jnp.where(
        odd_order[:, None, None, None, None, None], arrived[:, :, :, :, ::-1], arrived
    )
    raw_sums = jnp.einsum(
        "srbcpi,spij->sprbcj", swapped, legendre, preferred_element_type=jnp.float32
    )
    half_degrees = legendre.shape[3]
    degree = (
        2 * jnp.arange(half_degrees, dtype=jnp.int32)[None, :]
        + jnp.arange(2, dtype=jnp.int32)[:, None]
    )
    allowed = degree[None, :, :] >= orders[:, None, None]
    return jnp.where(allowed[:, :, None, None, None, :], raw_sums, 0.0).astype(jnp.bfloat16)


def general_path(field_grid, norm_gain, norm_bias, order_table, legendre):
    batch_size, chan_local, hemis, cycle_local, longitudes = field_grid.shape
    order_total = order_table.shape[0]
    values = field_grid.astype(jnp.float32)
    cell_count = hemis * cycle_local * lax.axis_size("ord") * longitudes
    partial_sum = jnp.sum(values, axis=(2, 3, 4))
    totals, squares = lax.psum((partial_sum, jnp.sum(values * values, axis=(2, 3, 4))), "ord")
    average = totals / cell_count
    spread = squares / cell_count - average * average
    centered = values - average[:, :, None, None, None]
    inverse_scale = lax.rsqrt(spread + 1e-05) * norm_gain[None, :]
    normed = (
        centered * inverse_scale[:, :, None, None, None] + norm_bias[None, :, None, None, None]
    ).astype(jnp.bfloat16)
    twiddle = slot_table(order_table, longitudes)
    flat_rows = normed.reshape(-1, longitudes)
    fourier = lax.dot_general(
        twiddle, flat_rows, (((0,), (1,)), ((), ())), preferred_element_type=jnp.float32
    )
    fourier = fourier.reshape(order_total, 2, batch_size, chan_local, hemis, cycle_local)
    north = fourier[:, :, :, :, 0]
    south = fourier[:, :, :, :, 1]
    halves = jnp.stack([north + south, north - south], axis=4).astype(jnp.bfloat16)
    slot_count = legendre.shape[0]
    channel_groups = lax.axis_size("ch")
    first_slot = (lax.axis_index("ord") * channel_groups + lax.axis_index("ch")) * slot_count
    own_orders = lax.dynamic_slice_in_dim(order_table, first_slot, slot_count)
    transform = partial(legendre_sums, legendre=legendre, orders=own_orders)
    arrived = lax.all_to_all(
        lax.all_to_all(halves, "ord", split_axis=0, concat_axis=5, tiled=True),
        "ch",
        split_axis=0,
        concat_axis=3,
        tiled=True,
    )
    return transform(arrived)


def turn(orders, jumps, length):
    product = orders * jumps.astype(jnp.float32)
    left = product - length * jnp.floor(product * (1.0 / length))
    half = (left - length // 2) * (math.pi / length)
    square = half * half
    sine = jnp.full(half.shape, -1.0 / math.factorial(11), jnp.float32)
    for power in (9, 7, 5, 3, 1):
        sine = sine * square + (1.0 if power % 4 == 1 else -1.0) / math.factorial(power)
    sine = sine * half
    cosine = jnp.full(half.shape, 1.0 / math.factorial(12), jnp.float32)
    for power in (10, 8, 6, 4, 2, 0):
        cosine = cosine * square + (1.0 if power % 4 == 0 else -1.0) / math.factorial(power)
    return 2.0 * sine * sine - 1.0, -2.0 * sine * cosine


def exchange_kernel(
    sizes, orders, gains, biases, field, legendre, out,
    grid, rows, packed, twiddle, signs, tsums, columns, sending, arrived, weights, wide, results,
    stats, centers, affine, message, reports, norms, scales, shifts,
    field_sem, report_out_sem, report_in_sem, send_sem, recv_sem, own_sem, weight_sem, out_sem,
):
    n_ord, n_ch, cell_count = sizes
    total = n_ord * n_ch
    fields, cycles, hemis, length = grid.shape
    groups = twiddle.shape[0]
    steps = packed.shape[0]
    slots = legendre.shape[0]
    per_phase = slots // groups
    tiles = rows.shape[0]
    local = gains.shape[0]
    own_ord, own_ch = lax.axis_index("ord"), lax.axis_index("ch")
    me = own_ord * n_ch + own_ch

    chunks = []
    begin = count = 0
    while begin + count < cycles:
        begin += count
        count = min(16 if begin else 8, cycles - begin)
        chunks.append((begin, count))

    def load(part):
        span = pl.ds(*chunks[part])
        return pltpu.make_async_copy(field.at[:, span], grid.at[:, span], field_sem.at[part])

    for part in range(len(chunks)):
        load(part).start()
    weight_load = pltpu.make_async_copy(legendre, weights, weight_sem)

    barrier = pltpu.get_barrier_semaphore()

    def greet(hop, carry):
        peer = lax.rem(me + hop, total)
        pl.semaphore_signal(
            barrier, inc=1, device_id=(peer // n_ch, lax.rem(peer, n_ch)), device_id_type=MESH
        )
        return carry

    lax.fori_loop(1, total, greet, 0)

    lane = lax.broadcasted_iota(jnp.int32, (GROUP, LANES), 1)

    def build(group):
        def put(device, carry):
            for at in range(per_phase):
                slot = device * slots + group * per_phase + at
                row = jnp.full((1, LANES), orders[slot], jnp.int32)
                columns[pl.ds(device * per_phase + at, 1), :] = row
            return carry

        lax.fori_loop(0, total, put, 0)
        order = columns[...].astype(jnp.float32)
        cos_fine, sin_fine = turn(order, lane, length)
        factor = 1.0 / math.sqrt(length)
        cos_fine, sin_fine = cos_fine * factor, sin_fine * factor
        jumps = jnp.where(lane == LANES - 1, length // 2, LANES * jnp.minimum(lane, tiles))
        cos_coarse, sin_coarse = turn(order, jumps, length)
        sign = jnp.where(cos_coarse[:, LANES - 1 :] < 0.0, -1.0, 1.0)
        signs[group] = jnp.broadcast_to(sign, (GROUP, LANES))
        for tile in range(tiles):
            span = slice(tile * LANES, (tile + 1) * LANES)
            cos_at, sin_at = cos_coarse[:, tile : tile + 1], sin_coarse[:, tile : tile + 1]
            twiddle[group, :GROUP, span] = (cos_at * cos_fine - sin_at * sin_fine).astype(jnp.bfloat16)
            twiddle[group, GROUP:, span] = (-(sin_at * cos_fine + cos_at * sin_fine)).astype(jnp.bfloat16)
        cell = lax.broadcasted_iota(jnp.int32, (LANES, tiles * LANES), 1)
        ones = jnp.where(cell < length, 1.0, 0.0).astype(jnp.bfloat16)
        tsums[group] = lax.dot_general(
            twiddle[group], ones, (((1,), (1,)), ((), ())), preferred_element_type=jnp.float32
        )

    for at in range(local):
        affine[at : at + 1, :] = jnp.full((1, LANES), gains[at], jnp.float32)
        affine[local + at : local + at + 1, :] = jnp.full((1, LANES), biases[at], jnp.float32)
    build(0)

    def collect(at, carry, begin, count):
        summed = jnp.zeros((2 * count, LANES), jnp.float32)
        squared = jnp.zeros((2 * count, LANES), jnp.float32)
        for tile in range(tiles):
            piece = grid[at, begin : begin + count, :, tile * LANES : min((tile + 1) * LANES, length)]
            across = piece.shape[2]
            piece = piece.reshape(hemis * count, across).astype(jnp.float32)
            if across < LANES:
                blank = jnp.zeros((hemis * count, LANES - across), jnp.float32)
                piece = jnp.concatenate([piece, blank], axis=1)
            rows[tile, pl.ds(at, hemis * count, stride=PITCH), :] = piece
            summed += piece
            squared += piece * piece
        summed = jnp.sum(summed, axis=0, keepdims=True)
        squared = jnp.sum(squared, axis=0, keepdims=True)
        if begin:
            summed += stats[pl.ds(at, 1), :]
            squared += stats[pl.ds(fields + at, 1), :]
        stats[pl.ds(at, 1), :] = summed
        stats[pl.ds(fields + at, 1), :] = squared
        return carry

    low = lane // fields % 2 == 0
    high = lane // (2 * fields) % 2 == 0

    def swap(mask, upper, lower, amount):
        return (
            jnp.where(mask, upper, pltpu.roll(lower, amount, 1)),
            jnp.where(mask, pltpu.roll(upper, LANES - amount, 1), lower),
        )

    sub = lax.broadcasted_iota(jnp.int32, (GROUP // 8, 8, LANES), 1)
    top = sub < per_phase

    def weave(first, second):
        first, second = first.reshape(GROUP // 8, 8, LANES), second.reshape(GROUP // 8, 8, LANES)
        return (
            jnp.where(top, first, pltpu.roll(second, per_phase, 1)),
            jnp.where(top, pltpu.roll(first, per_phase, 1), second),
        )

    def transform(phase, step, mode):
        spectrum = lax.dot_general(
            twiddle[phase], packed[step], (((1,), (1,)), ((), ())), preferred_element_type=jnp.float32
        )
        sign = signs[phase]
        sign = jnp.concatenate([sign, sign], axis=0)
        north, south = spectrum[:, :LANES], spectrum[:, LANES:] * sign
        scale = norms[mode, 0, :1, :]
        shift = tsums[phase] * norms[mode, 1, :1, :]
        even = (north + south) * scale + jnp.where(sign > 0.0, shift, 0.0)
        odd = (north - south) * scale + jnp.where(sign > 0.0, 0.0, shift)
        a, b, c, d = even[:GROUP], even[GROUP:], odd[:GROUP], odd[GROUP:]
        a, b = swap(low, a, b, fields)
        c, d = swap(low, c, d, fields)
        a, c = swap(high, a, c, 2 * fields)
        b, d = swap(high, b, d, 2 * fields)
        front, back = weave(a, b), weave(c, d)
        for side in range(2):
            both = jnp.concatenate([front[side], back[side]], axis=1)
            sending[phase, :, side, step] = both.astype(jnp.bfloat16)

    lone = n_ch // 2 * n_ord

    def toward(hop):
        ring = lax.rem(own_ch + hop // n_ord + n_ch // 2, n_ch)
        side = lax.rem(own_ord + hop, n_ord)
        return side, ring, side * n_ch + ring

    def send_step(phase, step):
        def send(hop, inner):
            side, ring, peer = toward(hop)
            pltpu.make_async_remote_copy(
                src_ref=sending.at[phase, peer // 2, lax.rem(peer, 2), step],
                dst_ref=arrived.at[phase, own_ch, own_ord, step],
                send_sem=send_sem.at[phase, peer],
                recv_sem=recv_sem.at[phase, me],
                device_id=(side, ring),
                device_id_type=MESH,
            ).start()
            return inner

        lax.fori_loop(0, lone, send, 0)
        lax.fori_loop(lone + 1, total, send, 0)

    def send_phase(phase):
        def send(hop, inner):
            side, ring, peer = toward(hop)
            pltpu.make_async_remote_copy(
                src_ref=sending.at[phase, peer // 2, lax.rem(peer, 2)],
                dst_ref=arrived.at[phase, own_ch, own_ord],
                send_sem=send_sem.at[phase, peer],
                recv_sem=recv_sem.at[phase, me],
                device_id=(side, ring),
                device_id_type=MESH,
            ).start()
            return inner

        lax.fori_loop(0, lone, send, 0)
        lax.fori_loop(lone + 1, total, send, 0)

    def pack(part):
        begin, count = chunks[part]
        load(part).wait()
        lax.fori_loop(0, fields, partial(collect, begin=begin, count=count), 0)

        def place_step(at, carry):
            step = begin // QUAD + at
            for hemi in range(hemis):
                for quarter in range(QUAD):
                    line = (at * QUAD + quarter) * hemis + hemi
                    span = pl.ds(pl.multiple_of(line * PITCH, 8), fields)
                    place = hemi * LANES + quarter * fields
                    for tile in range(tiles):
                        packed[step, place : place + fields, tile * LANES : (tile + 1) * LANES] = rows[
                            tile, span, :
                        ].astype(jnp.bfloat16)
            return carry

        lax.fori_loop(0, count // QUAD, place_step, 0)

    def first_phase(step, carry):
        transform(0, step, 0)
        send_step(0, step)
        return carry

    pack(0)
    sampled = hemis * chunks[0][1] * length
    center = jnp.sum(stats[:fields, :], axis=1, keepdims=True) / sampled
    center = jnp.broadcast_to(center, (fields, LANES))
    centers[...] = center
    across = jnp.concatenate([center] * QUAD, axis=0).T[:8]
    norms[0, 0] = jnp.ones((8, LANES), jnp.float32)
    norms[0, 1] = -2.0 * across

    pl.semaphore_wait(barrier, total - 1)
    early = chunks[0][1] // QUAD
    lax.fori_loop(0, early, first_phase, 0)

    for part in range(1, len(chunks)):
        pack(part)
    weight_load.start()

    local_sums = jnp.broadcast_to(jnp.sum(stats[...], axis=1, keepdims=True), (2 * fields, LANES))
    gathered = jnp.concatenate([local_sums, centers[...], affine[...]], axis=0).T
    message[...] = gathered[:1]
    reports[me] = gathered[:1]

    def report(hop):
        peer = lax.rem(me + hop, total)
        return pltpu.make_async_remote_copy(
            src_ref=message,
            dst_ref=reports.at[me],
            send_sem=report_out_sem.at[peer],
            recv_sem=report_in_sem.at[me],
            device_id=(peer // n_ch, lax.rem(peer, n_ch)),
            device_id_type=MESH,
        )

    def reported(peer):
        return pltpu.make_async_remote_copy(
            src_ref=message,
            dst_ref=reports.at[peer],
            send_sem=report_out_sem.at[peer],
            recv_sem=report_in_sem.at[peer],
            device_id=(peer // n_ch, lax.rem(peer, n_ch)),
            device_id_type=MESH,
        )

    def tell(hop, carry):
        report(hop).start()
        return carry

    lax.fori_loop(1, total, tell, 0)
    lax.fori_loop(early, steps, first_phase, 0)

    spot = lax.broadcasted_iota(jnp.int32, (8, LANES), 1)

    def tile_lanes(values, start, width):
        values = jnp.where((spot >= start) & (spot < start + width), values, 0.0)
        while width < LANES:
            values = values + pltpu.roll(values, width, 1)
            width *= 2
        return values

    def affine_of(source):
        summed = reports[source]
        for at in range(1, n_ord):
            summed = summed + reports[at * n_ch + source]
        summed = jnp.broadcast_to(summed, (8, LANES))
        own = jnp.broadcast_to(reports[source], (8, LANES))
        average = tile_lanes(summed, 0, fields) / cell_count
        spread = tile_lanes(summed, fields, fields) / cell_count - average * average
        gain = tile_lanes(own, 3 * fields, local)
        offset = tile_lanes(own, 3 * fields + local, local)
        return average, lax.rsqrt(spread + 1e-05) * gain, offset

    for hop in range(1, n_ord):
        reported(lax.rem(own_ord + hop, n_ord) * n_ch + own_ch).wait()
    average, scale, offset = affine_of(own_ch)
    norms[1, 0] = scale
    norms[1, 1] = 2.0 * (offset - average * scale)

    def later_phase(phase, carry):
        build(phase)

        def one(step, inner):
            transform(phase, step, 1)
            return inner

        lax.fori_loop(0, steps, one, 0)
        send_phase(phase)
        return carry

    lax.fori_loop(1, groups, later_phase, 0)

    def own_copy(phase):
        return pltpu.make_async_copy(
            sending.at[phase, me // 2, lax.rem(me, 2)], arrived.at[phase, own_ch, own_ord], own_sem.at[phase]
        )

    def out_copy(phase):
        return pltpu.make_async_copy(
            results.at[lax.rem(phase, 2)], out.at[pl.ds(phase * per_phase, per_phase)], out_sem.at[phase]
        )

    for phase in range(groups):
        own_copy(phase).start()
    weight_load.wait()

    def heard(hop, carry):
        others = n_ch - 1
        ring = lax.rem(own_ch + 1 + lax.rem(hop, others), n_ch)
        reported(hop // others * n_ch + ring).wait()
        return carry

    lax.fori_loop(0, n_ord * (n_ch - 1), heard, 0)
    for source in range(n_ch):
        average, scale, offset = affine_of(source)
        scales[source] = scale
        for at in range(n_ord):
            center = tile_lanes(jnp.broadcast_to(reports[at * n_ch + source], (8, LANES)), 2 * fields, fields)
            shift = 2.0 * ((center - average) * scale + offset)
            shifts[source, at * cycles : (at + 1) * cycles, :] = jnp.broadcast_to(shift[:1], (cycles, LANES))

    batch = results.shape[4]
    half = LANES // 2
    depth = n_ord * cycles

    def conclude(phase, carry, raw=False):
        def finish(hop, inner):
            peer = lax.rem(me + hop, total)
            pltpu.make_async_remote_copy(
                src_ref=sending.at[phase, peer // 2, lax.rem(peer, 2)],
                dst_ref=arrived.at[phase, lax.rem(peer, n_ch), peer // n_ch],
                send_sem=send_sem.at[phase, peer],
                recv_sem=recv_sem.at[phase, peer],
                device_id=(peer // n_ch, lax.rem(peer, n_ch)),
                device_id_type=MESH,
            ).wait()
            return inner

        lax.fori_loop(1, total, finish, 0)
        own_copy(phase).wait()

        @pl.when(phase >= 2)
        def _():
            out_copy(phase - 2).wait()

        for source in range(n_ch):
            wide[source] = arrived[phase, source].astype(jnp.float32).reshape(depth * per_phase, LANES)

        def analyze(at, inner):
            slot = phase * per_phase + at
            order = orders[me * slots + slot]
            line = spot[:1]
            if raw:
                row = me * per_phase + at
                real, imag = tsums[0, pl.ds(row, 1), :], tsums[0, pl.ds(GROUP + row, 1), :]
                sign = signs[0, pl.ds(row, 1), :]
                sums = jnp.where(line // fields % 2 == 0, real, imag)
                sums = jnp.where(jnp.where(line < half, sign, -sign) > 0.0, sums, 0.0)

            def turned_rows(source):
                piece = wide[source, pl.ds(at, depth, stride=per_phase), :]
                if raw:
                    piece = piece * scales[source, :1, :] + shifts[source] * sums
                return piece.T.astype(jnp.bfloat16)

            turned = [turned_rows(source) for source in range(n_ch)]
            for parity in range(2):
                left = jnp.concatenate([t[parity * half : (parity + 1) * half] for t in turned], axis=0)
                product = jnp.dot(left, weights[slot, parity], preferred_element_type=jnp.float32)
                degree = 2 * lax.broadcasted_iota(jnp.int32, product.shape, 1) + parity
                product = jnp.where(degree >= order, product, 0.0).astype(jnp.bfloat16)
                for source in range(n_ch):
                    results[lax.rem(phase, 2), at, parity, :, :, source * local : (source + 1) * local, :] = product[
                        source * half : (source + 1) * half
                    ].reshape(2, batch, local, product.shape[1])
            return inner

        lax.fori_loop(0, per_phase, analyze, 0)
        out_copy(phase).start()
        return carry

    conclude(0, 0, raw=True)
    lax.fori_loop(1, groups, conclude, 0)
    for phase in range(groups - 2, groups):
        out_copy(phase).wait()


def emit_kernel(source, target, held, in_sem, out_sem):
    count = held.shape[0]

    def load(at):
        return pltpu.make_async_copy(source.at[at], held.at[at], in_sem.at[at])

    def store(at):
        return pltpu.make_async_copy(held.at[at], target.at[at], out_sem.at[at])

    for at in range(count):
        load(at).start()
    for at in range(count):
        load(at).wait()
        store(at).start()
    for at in range(count):
        store(at).wait()


def kernel_path(field_grid, norm_gain, norm_bias, order_table, legendre):
    batch, local, hemis, cycles, length = field_grid.shape
    n_ord, n_ch = lax.axis_size("ord"), lax.axis_size("ch")
    order_total, slots = order_table.shape[0], legendre.shape[0]
    fields = batch * local
    groups = order_total // GROUP
    tiles = -(-length // LANES)
    steps = cycles // QUAD
    total = n_ord * n_ch
    per_phase = slots // groups
    half_degrees = legendre.shape[3]
    smem = pl.BlockSpec(memory_space=pltpu.SMEM)
    hbm = pl.BlockSpec(memory_space=pltpu.HBM)
    depth = n_ord * cycles
    result = (2, 2, batch, n_ch * local, half_degrees)
    summed = pl.pallas_call(
        partial(exchange_kernel, (n_ord, n_ch, hemis * cycles * n_ord * length)),
        out_shape=jax.ShapeDtypeStruct((slots,) + result, jnp.bfloat16),
        in_specs=[smem, smem, smem, hbm, hbm],
        out_specs=hbm,
        scratch_shapes=[
            pltpu.VMEM((fields, cycles, hemis, length), jnp.bfloat16),
            pltpu.VMEM((tiles, hemis * 16 * PITCH, LANES), jnp.float32),
            pltpu.VMEM((steps, hemis * LANES, tiles * LANES), jnp.bfloat16),
            pltpu.VMEM((groups, 2 * GROUP, tiles * LANES), jnp.bfloat16),
            pltpu.VMEM((groups, GROUP, LANES), jnp.float32),
            pltpu.VMEM((groups, 2 * GROUP, LANES), jnp.float32),
            pltpu.VMEM((GROUP, LANES), jnp.int32),
            pltpu.VMEM((groups, total // 2, 2, steps, QUAD * per_phase, LANES), jnp.bfloat16),
            pltpu.VMEM((groups, n_ch, n_ord, steps, QUAD * per_phase, LANES), jnp.bfloat16),
            pltpu.VMEM(legendre.shape, jnp.bfloat16),
            pltpu.VMEM((n_ch, depth * per_phase, LANES), jnp.float32),
            pltpu.VMEM((2, per_phase) + result, jnp.bfloat16),
            pltpu.VMEM((2 * fields, LANES), jnp.float32),
            pltpu.VMEM((fields, LANES), jnp.float32),
            pltpu.VMEM((2 * local, LANES), jnp.float32),
            pltpu.VMEM((1, LANES), jnp.float32),
            pltpu.VMEM((total, 1, LANES), jnp.float32),
            pltpu.VMEM((2, 2, 8, LANES), jnp.float32),
            pltpu.VMEM((n_ch, 8, LANES), jnp.float32),
            pltpu.VMEM((n_ch, depth, LANES), jnp.float32),
            pltpu.SemaphoreType.DMA((8,)),
            pltpu.SemaphoreType.DMA((total,)),
            pltpu.SemaphoreType.DMA((total,)),
            pltpu.SemaphoreType.DMA((groups, total)),
            pltpu.SemaphoreType.DMA((groups, total)),
            pltpu.SemaphoreType.DMA((groups,)),
            pltpu.SemaphoreType.DMA,
            pltpu.SemaphoreType.DMA((groups,)),
        ],
        compiler_params=pltpu.CompilerParams(
            collective_id=0, has_side_effects=True, vmem_limit_bytes=63 * 2**20
        ),
        name="spectral_analysis",
    )(order_table, norm_gain, norm_bias, field_grid.transpose(0, 1, 3, 2, 4).reshape(fields, cycles, hemis, length), legendre)
    return pl.pallas_call(
        emit_kernel,
        out_shape=jax.ShapeDtypeStruct(summed.shape, summed.dtype),
        in_specs=[hbm],
        out_specs=hbm,
        scratch_shapes=[
            pltpu.VMEM(summed.shape, summed.dtype),
            pltpu.SemaphoreType.DMA((slots,)),
            pltpu.SemaphoreType.DMA((slots,)),
        ],
        name="emit_result",
    )(summed)


def on_device(field_grid, norm_gain, norm_bias, order_table, legendre):
    batch, local, hemis, cycles, _ = field_grid.shape
    fits = (
        batch == 2
        and batch * local * QUAD == LANES
        and hemis == 2
        and cycles % QUAD == 0
        and legendre.shape[0] == 16
        and order_table.shape[0] == 4 * GROUP
        and field_grid.shape[4] <= LANES * (LANES - 1)
        and field_grid.shape[4] % 2 == 0
    )
    path = kernel_path if fits else general_path
    return path(field_grid, norm_gain, norm_bias, order_table, legendre)


def solution(mesh):
    placed = (
        P(None, "ch", None, "ord", None),
        P("ch"),
        P("ch"),
        P(),
        P(("ord", "ch"), None, None, None),
    )
    return jax.shard_map(
        on_device,
        mesh=mesh,
        in_specs=placed,
        out_specs=P(("ord", "ch"), None, None, None, None, None),
        check_vma=False,
    )
```

profile of v0, /device:TPU:9, one launch (start us, length us, event | category | flops | bytes accessed | tf_op | source)
XLA Modules:
  0.0 155.3 jit_solution(9114145380694363932)
XLA Ops:
  0.0 149.8 %spectral_analysis.1.source = bf16[16,2,2,2,64,360]{5,4,3,2,1,0:T(8,128)(2,1)} custom-call(s32[512]{0:T(512)} %orders.1, f32[16]{0:T(128)} %gains.1, f32[16]{0:T(128)} %biases.1, bf16[32,44,2,1440]{3,2,1,0:T(2,128)(2,1)} %bitcast.3, bf16[16,2,352,360]{3,2,1,0:T(8,128)(2,1)} %legendre.1), custom_call_target="tpu_custom_call" | custom-call | tf_op jit(solution)/shard_map/spectral_analysis/pallas_call | solution.py:520
  149.8 5.5 %emit_result.1 = bf16[16,2,2,2,64,360]{5,4,3,2,1,0:T(8,128)(2,1)} custom-call(bf16[16,2,2,2,64,360]{5,4,3,2,1,0:T(8,128)(2,1)} %spectral_analysis.1.source), custom_call_target="tpu_custom_call" | custom-call | tf_op jit(solution)/shard_map/emit_result/pallas_call | solution.py:560
where the time goes:
time: 155 us
  Pallas kernels  155 us (100%)
    pallas_call x1, Pallas kernels, kernel_path(): pl.pallas_call(partial(exchange_kernel, (n_ord, n_ch, hemis * cycles * n_...  150 us
    pallas_call x1, Pallas kernels, kernel_path(): pl.pallas_call(emit_kernel, out_shape=jax.ShapeDtypeStruct(summed.shape,...  5.48 us

commit v1 on v0

--- a/solution.py
+++ b/solution.py
@@ -13,6 +13,7 @@
 GROUP = 128
 QUAD = 4
 PITCH = 40
+RAW = 2
 
 
 def slot_table(orders, length):
@@ -96,9 +97,9 @@
 
 def exchange_kernel(
     sizes, orders, gains, biases, field, legendre, out,
-    grid, rows, packed, twiddle, signs, tsums, columns, sending, arrived, weights, wide, results,
+    grid, rows, packed, twiddle, signs, tsums, columns, sending, arrived, weights, wide, left,
     stats, centers, affine, message, reports, norms, scales, shifts,
-    field_sem, report_out_sem, report_in_sem, send_sem, recv_sem, own_sem, weight_sem, out_sem,
+    field_sem, report_out_sem, report_in_sem, send_sem, recv_sem, own_sem, weight_sem,
 ):
     n_ord, n_ch, cell_count = sizes
     total = n_ord * n_ch
@@ -116,7 +117,7 @@
     begin = count = 0
     while begin + count < cycles:
         begin += count
-        count = min(16 if begin else 8, cycles - begin)
+        count = min(max(len(chunks), 1) * QUAD, 4 * QUAD, cycles - begin)
         chunks.append((begin, count))
 
     def load(part):
@@ -237,19 +238,26 @@
 
     lone = n_ch // 2 * n_ord
 
+    def partner(turned):
+        low_bit = lax.rem(own_ch + turned, 2)
+        high_bit = lax.rem(own_ch // 2 + turned // 2, 2)
+        return 2 * high_bit + low_bit
+
     def toward(hop):
-        ring = lax.rem(own_ch + hop // n_ord + n_ch // 2, n_ch)
+        ring = partner(lax.rem(hop // n_ord + n_ch // 2, n_ch))
         side = lax.rem(own_ord + hop, n_ord)
         return side, ring, side * n_ch + ring
 
-    def send_step(phase, step):
+    def send_part(part):
+        span = pl.ds(chunks[part][0] // QUAD, chunks[part][1] // QUAD)
+
         def send(hop, inner):
             side, ring, peer = toward(hop)
             pltpu.make_async_remote_copy(
-                src_ref=sending.at[phase, peer // 2, lax.rem(peer, 2), step],
-                dst_ref=arrived.at[phase, own_ch, own_ord, step],
-                send_sem=send_sem.at[phase, peer],
-                recv_sem=recv_sem.at[phase, me],
+                src_ref=sending.at[0, peer // 2, lax.rem(peer, 2), span],
+                dst_ref=arrived.at[0, own_ch, own_ord, span],
+                send_sem=send_sem.at[0, peer],
+                recv_sem=recv_sem.at[0, me],
                 device_id=(side, ring),
                 device_id_type=MESH,
             ).start()
@@ -296,7 +304,6 @@
 
     def first_phase(step, carry):
         transform(0, step, 0)
-        send_step(0, step)
         return carry
 
     pack(0)
@@ -309,11 +316,13 @@
     norms[0, 1] = -2.0 * across
 
     pl.semaphore_wait(barrier, total - 1)
-    early = chunks[0][1] // QUAD
-    lax.fori_loop(0, early, first_phase, 0)
-
+    lax.fori_loop(0, chunks[0][1] // QUAD, first_phase, 0)
+    send_part(0)
     for part in range(1, len(chunks)):
         pack(part)
+        begin, count = chunks[part]
+        lax.fori_loop(begin // QUAD, (begin + count) // QUAD, first_phase, 0)
+        send_part(part)
     weight_load.start()
 
     local_sums = jnp.broadcast_to(jnp.sum(stats[...], axis=1, keepdims=True), (2 * fields, LANES))
@@ -347,7 +356,6 @@
         return carry
 
     lax.fori_loop(1, total, tell, 0)
-    lax.fori_loop(early, steps, first_phase, 0)
 
     spot = lax.broadcasted_iota(jnp.int32, (8, LANES), 1)
 
@@ -370,33 +378,28 @@
         offset = tile_lanes(own, 3 * fields + local, local)
         return average, lax.rsqrt(spread + 1e-05) * gain, offset
 
+    def later_phase(phase, carry, mode):
+        build(phase)
+
+        def one(step, inner):
+            transform(phase, step, mode)
+            return inner
+
+        lax.fori_loop(0, steps, one, 0)
+        send_phase(phase)
+        return carry
+
+    lax.fori_loop(1, RAW, partial(later_phase, mode=0), 0)
     for hop in range(1, n_ord):
         reported(lax.rem(own_ord + hop, n_ord) * n_ch + own_ch).wait()
     average, scale, offset = affine_of(own_ch)
     norms[1, 0] = scale
     norms[1, 1] = 2.0 * (offset - average * scale)
-
-    def later_phase(phase, carry):
-        build(phase)
-
-        def one(step, inner):
-            transform(phase, step, 1)
-            return inner
-
-        lax.fori_loop(0, steps, one, 0)
-        send_phase(phase)
-        return carry
-
-    lax.fori_loop(1, groups, later_phase, 0)
+    lax.fori_loop(RAW, groups, partial(later_phase, mode=1), 0)
 
     def own_copy(phase):
         return pltpu.make_async_copy(
             sending.at[phase, me // 2, lax.rem(me, 2)], arrived.at[phase, own_ch, own_ord], own_sem.at[phase]
-        )
-
-    def out_copy(phase):
-        return pltpu.make_async_copy(
-            results.at[lax.rem(phase, 2)], out.at[pl.ds(phase * per_phase, per_phase)], out_sem.at[phase]
         )
 
     for phase in range(groups):
@@ -418,88 +421,78 @@
             shift = 2.0 * ((center - average) * scale + offset)
             shifts[source, at * cycles : (at + 1) * cycles, :] = jnp.broadcast_to(shift[:1], (cycles, LANES))
 
-    batch = results.shape[4]
+    batch = out.shape[3]
     half = LANES // 2
     depth = n_ord * cycles
 
     def conclude(phase, carry, raw=False):
-        def finish(hop, inner):
-            peer = lax.rem(me + hop, total)
-            pltpu.make_async_remote_copy(
-                src_ref=sending.at[phase, peer // 2, lax.rem(peer, 2)],
-                dst_ref=arrived.at[phase, lax.rem(peer, n_ch), peer // n_ch],
-                send_sem=send_sem.at[phase, peer],
-                recv_sem=recv_sem.at[phase, peer],
-                device_id=(peer // n_ch, lax.rem(peer, n_ch)),
-                device_id_type=MESH,
-            ).wait()
-            return inner
-
-        lax.fori_loop(1, total, finish, 0)
         own_copy(phase).wait()
 
-        @pl.when(phase >= 2)
-        def _():
-            out_copy(phase - 2).wait()
-
-        for source in range(n_ch):
-            wide[source] = arrived[phase, source].astype(jnp.float32).reshape(depth * per_phase, LANES)
+        line = spot[:1]
+        for turned in range(n_ch):
+            source = partner(turned)
+
+            def receive(at, inner, source=source, turned=turned):
+                peer = lax.rem(own_ord + at, n_ord) * n_ch + source
+                pltpu.make_async_remote_copy(
+                    src_ref=sending.at[phase, peer // 2, lax.rem(peer, 2)],
+                    dst_ref=arrived.at[phase, source, peer // n_ch],
+                    send_sem=send_sem.at[phase, peer],
+                    recv_sem=recv_sem.at[phase, peer],
+                    device_id=(peer // n_ch, source),
+                    device_id_type=MESH,
+                ).wait_recv()
+                return inner
+
+            lax.fori_loop(0 if turned else 1, n_ord, receive, 0)
+            wide[turned % 2] = arrived[phase, source].astype(jnp.float32).reshape(depth * per_phase, LANES)
+            for at in range(per_phase):
+                piece = wide[turned % 2, pl.ds(at, depth, stride=per_phase), :]
+                if raw:
+                    row = me * per_phase + at
+                    real, imag = tsums[phase, pl.ds(row, 1), :], tsums[phase, pl.ds(GROUP + row, 1), :]
+                    sign = signs[phase, pl.ds(row, 1), :]
+                    sums = jnp.where(line // fields % 2 == 0, real, imag)
+                    sums = jnp.where(jnp.where(line < half, sign, -sign) > 0.0, sums, 0.0)
+                    piece = piece * scales[source, :1, :] + shifts[source] * sums
+                piece = piece.T.astype(jnp.bfloat16)
+                span = pl.ds(pl.multiple_of(source * half, half), half)
+                for parity in range(2):
+                    left[at, parity, span, :] = piece[parity * half : (parity + 1) * half]
 
         def analyze(at, inner):
             slot = phase * per_phase + at
             order = orders[me * slots + slot]
-            line = spot[:1]
-            if raw:
-                row = me * per_phase + at
-                real, imag = tsums[0, pl.ds(row, 1), :], tsums[0, pl.ds(GROUP + row, 1), :]
-                sign = signs[0, pl.ds(row, 1), :]
-                sums = jnp.where(line // fields % 2 == 0, real, imag)
-                sums = jnp.where(jnp.where(line < half, sign, -sign) > 0.0, sums, 0.0)
-
-            def turned_rows(source):
-                piece = wide[source, pl.ds(at, depth, stride=per_phase), :]
-                if raw:
-                    piece = piece * scales[source, :1, :] + shifts[source] * sums
-                return piece.T.astype(jnp.bfloat16)
-
-            turned = [turned_rows(source) for source in range(n_ch)]
             for parity in range(2):
-                left = jnp.concatenate([t[parity * half : (parity + 1) * half] for t in turned], axis=0)
-                product = jnp.dot(left, weights[slot, parity], preferred_element_type=jnp.float32)
+                product = jnp.dot(left[at, parity], weights[slot, parity], preferred_element_type=jnp.float32)
                 degree = 2 * lax.broadcasted_iota(jnp.int32, product.shape, 1) + parity
                 product = jnp.where(degree >= order, product, 0.0).astype(jnp.bfloat16)
                 for source in range(n_ch):
-                    results[lax.rem(phase, 2), at, parity, :, :, source * local : (source + 1) * local, :] = product[
+                    out[slot, parity, :, :, source * local : (source + 1) * local, :] = product[
                         source * half : (source + 1) * half
                     ].reshape(2, batch, local, product.shape[1])
             return inner
 
         lax.fori_loop(0, per_phase, analyze, 0)
-        out_copy(phase).start()
-        return carry
-
-    conclude(0, 0, raw=True)
-    lax.fori_loop(1, groups, conclude, 0)
-    for phase in range(groups - 2, groups):
-        out_copy(phase).wait()
-
-
-def emit_kernel(source, target, held, in_sem, out_sem):
-    count = held.shape[0]
-
-    def load(at):
-        return pltpu.make_async_copy(source.at[at], held.at[at], in_sem.at[at])
-
-    def store(at):
-        return pltpu.make_async_copy(held.at[at], target.at[at], out_sem.at[at])
-
-    for at in range(count):
-        load(at).start()
-    for at in range(count):
-        load(at).wait()
-        store(at).start()
-    for at in range(count):
-        store(at).wait()
+        return carry
+
+    lax.fori_loop(0, RAW, partial(conclude, raw=True), 0)
+    lax.fori_loop(RAW, groups, conclude, 0)
+
+    def drain(at, carry):
+        phase, hop = at // (total - 1), 1 + lax.rem(at, total - 1)
+        peer = lax.rem(me + hop, total)
+        pltpu.make_async_remote_copy(
+            src_ref=sending.at[phase, peer // 2, lax.rem(peer, 2)],
+            dst_ref=arrived.at[phase, own_ch, own_ord],
+            send_sem=send_sem.at[phase, peer],
+            recv_sem=recv_sem.at[phase, peer],
+            device_id=(peer // n_ch, lax.rem(peer, n_ch)),
+            device_id_type=MESH,
+        ).wait_send()
+        return carry
+
+    lax.fori_loop(0, groups * (total - 1), drain, 0)
 
 
 def kernel_path(field_grid, norm_gain, norm_bias, order_table, legendre):
@@ -515,13 +508,14 @@
     half_degrees = legendre.shape[3]
     smem = pl.BlockSpec(memory_space=pltpu.SMEM)
     hbm = pl.BlockSpec(memory_space=pltpu.HBM)
+    vmem = pl.BlockSpec(memory_space=pltpu.VMEM)
     depth = n_ord * cycles
     result = (2, 2, batch, n_ch * local, half_degrees)
     summed = pl.pallas_call(
         partial(exchange_kernel, (n_ord, n_ch, hemis * cycles * n_ord * length)),
-        out_shape=jax.ShapeDtypeStruct((slots,) + result, jnp.bfloat16),
+        out_shape=pltpu.VMEM((slots,) + result, jnp.bfloat16),
         in_specs=[smem, smem, smem, hbm, hbm],
-        out_specs=hbm,
+        out_specs=vmem,
         scratch_shapes=[
             pltpu.VMEM((fields, cycles, hemis, length), jnp.bfloat16),
             pltpu.VMEM((tiles, hemis * 16 * PITCH, LANES), jnp.float32),
@@ -533,8 +527,8 @@
             pltpu.VMEM((groups, total // 2, 2, steps, QUAD * per_phase, LANES), jnp.bfloat16),
             pltpu.VMEM((groups, n_ch, n_ord, steps, QUAD * per_phase, LANES), jnp.bfloat16),
             pltpu.VMEM(legendre.shape, jnp.bfloat16),
-            pltpu.VMEM((n_ch, depth * per_phase, LANES), jnp.float32),
-            pltpu.VMEM((2, per_phase) + result, jnp.bfloat16),
+            pltpu.VMEM((2, depth * per_phase, LANES), jnp.float32),
+            pltpu.VMEM((per_phase, 2, n_ch * LANES // 2, depth), jnp.bfloat16),
             pltpu.VMEM((2 * fields, LANES), jnp.float32),
             pltpu.VMEM((fields, LANES), jnp.float32),
             pltpu.VMEM((2 * local, LANES), jnp.float32),
@@ -550,31 +544,20 @@
             pltpu.SemaphoreType.DMA((groups, total)),
             pltpu.SemaphoreType.DMA((groups,)),
             pltpu.SemaphoreType.DMA,
-            pltpu.SemaphoreType.DMA((groups,)),
         ],
         compiler_params=pltpu.CompilerParams(
-            collective_id=0, has_side_effects=True, vmem_limit_bytes=63 * 2**20
+            collective_id=0, has_side_effects=True, vmem_limit_bytes=56 * 2**20
         ),
         name="spectral_analysis",
     )(order_table, norm_gain, norm_bias, field_grid.transpose(0, 1, 3, 2, 4).reshape(fields, cycles, hemis, length), legendre)
-    return pl.pallas_call(
-        emit_kernel,
-        out_shape=jax.ShapeDtypeStruct(summed.shape, summed.dtype),
-        in_specs=[hbm],
-        out_specs=hbm,
-        scratch_shapes=[
-            pltpu.VMEM(summed.shape, summed.dtype),
-            pltpu.SemaphoreType.DMA((slots,)),
-            pltpu.SemaphoreType.DMA((slots,)),
-        ],
-        name="emit_result",
-    )(summed)
+    return summed
 
 
 def on_device(field_grid, norm_gain, norm_bias, order_table, legendre):
     batch, local, hemis, cycles, _ = field_grid.shape
     fits = (
         batch == 2
+        and lax.axis_size("ch") == 4
         and batch * local * QUAD == LANES
         and hemis == 2
         and cycles % QUAD == 0

time: 155 us -> 147 us (0.948)
  Pallas kernels: 155 us -> 144 us
  local copies, waits for them, and re-layouts: 0 us -> 2.71 us
    pallas_call x1, Pallas kernels: 150 us -> 144 us  [kernel_path(): pl.pallas_call(partial(exchange_kernel, (n_ord, n_ch, hemis * cycles * n_...]
    pallas_call x1 -> x0, Pallas kernels: 5.48 us -> none  [kernel_path(): pl.pallas_call(emit_kernel, out_shape=jax.ShapeDtypeStruct(summed.shape,...]
    unnamed x0 -> x1, local copies, waits for them, and re-layouts: none -> 2.71 us
where the time goes in v1:
time: 147 us
  Pallas kernels  144 us (98%)
  local copies, waits for them, and re-layouts  2.71 us (2%)
    pallas_call x1, Pallas kernels, kernel_path(): pl.pallas_call(partial(exchange_kernel, (n_ord, n_ch, hemis * cycles * n_...  144 us

profile of v1, /device:TPU:9, one launch (start us, length us, event | category | flops | bytes accessed | tf_op | source)
XLA Modules:
  0.0 146.8 jit_solution(3859172704673111908)
XLA Ops:
  0.0 144.1 %spectral_analysis.1 = bf16[16,2,2,2,64,360]{5,4,3,2,1,0:T(8,128)(2,1)S(1)} custom-call(s32[512]{0:T(512)} %orders.1, f32[16]{0:T(128)} %gains.1, f32[16]{0:T(128)} %biases.1, bf16[32,44,2,1440]{3,2,1,0:T(2,128)(2,1)} %bitcast.3, bf16[16,2,352,360]{3,2,1,0:T(8,128)(2,1)} %legendre.1), custom_call_target="tpu_custom_call" | custom-call | tf_op jit(solution)/shard_map/spectral_analysis/pallas_call | solution.py:514
  144.1 2.7 %copy.7 = bf16[16,2,2,2,64,360]{5,4,3,2,1,0:T(8,128)(2,1)} copy(bf16[16,2,2,2,64,360]{5,4,3,2,1,0:T(8,128)(2,1)S(1)} %spectral_analysis.1) | data formatting | bytes 11796480
